TPU v7x, 32 devices: a whole 2x2x4 slice. The times are simulated.
32 devices in a mesh: tm: 16 (over z, y, x), space: 2 (over core).
Axes of the slice: x: 2, y: 2, z: 4, core: 2. Of those that a mesh axis runs over, the one named last changes fastest.
Arguments:
- features: bfloat16 [16, 16, 16, 256], P('tm', 'space'), may hold values from -6 to 6
- masks: int32 [16, 16, 16], P('tm', 'space'), may hold values from 0 to 1
- w_pix: bfloat16 [256, 256], replicated, may hold values from -0.375 to 0.375
- mask_embed: bfloat16 [256], replicated, may hold values from -4 to 4
- w_conv: bfloat16 [3, 3, 256, 256], replicated, may hold values from -0.125 to 0.125
- w_out: bfloat16 [256, 64], replicated, may hold values from -0.375 to 0.375
- w_ptr: bfloat16 [256, 256], replicated, may hold values from -0.375 to 0.375
- w_query: bfloat16 [256, 256], replicated, may hold values from -1 to 1
- w_key: bfloat16 [64, 256], replicated, may hold values from -0.75 to 0.75
- w_value: bfloat16 [64, 256], replicated, may hold values from -0.75 to 0.75
- w_proj: bfloat16 [256, 256], replicated, may hold values from -0.375 to 0.375
- mem_tpos: bfloat16 [3, 64], replicated, may hold values from -120 to 120
- ptr_tpos: bfloat16 [16, 256], replicated, may hold values from -4 to 4
- empty_memory: bfloat16 [64], replicated, may hold values from -4 to 4
Outputs:
- attended: bfloat16 [16, 16, 16, 256], P('tm', 'space')
- memory: bfloat16 [16, 16, 1024], P('tm', 'space')
- pointers: bfloat16 [16, 256], P('tm')
All inputs are finite; a program needn't handle non-finite values.
Results may differ from a plain program's by a relative error of at most 0.015.
The roundings to bfloat16 on the way count: a program that leaves them out, or rounds other values in their place, can miss the bound.
Values may be sent and summed in bfloat16 or wider, within the bound.
A program may use at most 128 MiB of HBM per device.

v0:
```python
import jax
import jax.numpy as jnp
from jax import lax
from jax.sharding import PartitionSpec as P

MEMS = 3
POINTERS = 16


def from_behind(block, axis, distance):
    devices = range(lax.axis_size(axis))
    route = [(i - distance, i) for i in devices if i - distance in devices]
    return lax.ppermute(block, axis, route)


def with_halo(block, sides, width):
    for axis, dim in sides:
        count = lax.axis_size(axis)
        forward = [(i, i + 1) for i in range(count - 1)]
        backward = [(target, source) for source, target in forward]
        low = lax.ppermute(
            lax.slice_in_dim(block, block.shape[dim] - width, None, axis=dim), axis, forward
        )
        high = lax.ppermute(lax.slice_in_dim(block, 0, width, axis=dim), axis, backward)
        block = jnp.concatenate([low, block, high], axis=dim)
    return block


def fetch_earlier(carried, hop_count):
    pieces = []
    for step_index in range(hop_count):
        pieces.append(from_behind(carried, "tm", step_index + 1))
    return jnp.concatenate(pieces[::-1], axis=0)


def attend(query, blocks):
    scores = []
    row_top = None
    for key_rows, value_rows, is_valid in blocks:
        block_scores = lax.dot_general(
            query, key_rows, (((1,), (1,)), ((), ())), preferred_element_type=jnp.float32
        )
        block_scores = jnp.where(is_valid, block_scores, -jnp.inf)
        scores.append(block_scores)
        block_top = jnp.max(block_scores, axis=1, keepdims=True)
        row_top = block_top if row_top is None else jnp.maximum(row_top, block_top)
    row_total = jnp.zeros_like(row_top)
    for block_scores in scores:
        row_total = row_total + jnp.sum(jnp.exp(block_scores - row_top), axis=1, keepdims=True)
    mixed_sum = jnp.zeros((query.shape[0], blocks[0][1].shape[1]), jnp.float32)
    for block_scores, block in zip(scores, blocks):
        weights = (jnp.exp(block_scores - row_top) / row_total).astype(jnp.bfloat16)
        mixed_sum = mixed_sum + jnp.dot(weights, block[1], preferred_element_type=jnp.float32)
    return mixed_sum.astype(jnp.bfloat16)


def body(
    features,
    masks,
    w_pix,
    mask_embed,
    w_conv,
    w_out,
    w_ptr,
    w_query,
    w_key,
    w_value,
    w_proj,
    mem_tpos,
    ptr_tpos,
    empty_memory,
):
    frames_dev, rows_dev, columns, model_dim = features.shape
    mem_dim = w_key.shape[0]
    ptr_tok = model_dim // mem_dim
    band_tokens = rows_dev * columns
    flat_rows = features.reshape(frames_dev * band_tokens, model_dim)
    mask_rows = masks.reshape(frames_dev * band_tokens, 1).astype(jnp.float32)
    joined_map = (
        jnp.dot(flat_rows, w_pix, preferred_element_type=jnp.float32)
        + mask_rows * mask_embed.astype(jnp.float32)
    ).astype(jnp.bfloat16)
    joined_map = joined_map.reshape(frames_dev, rows_dev, columns, model_dim)
    padded = with_halo(joined_map, (("space", 1),), 1)
    padded = jnp.pad(padded, ((0, 0), (0, 0), (1, 1), (0, 0)))
    conv_sum = jnp.zeros((frames_dev * band_tokens, model_dim), jnp.float32)
    for row_tap in range(3):
        for col_tap in range(3):
            window_rows = padded[
                :, row_tap : row_tap + rows_dev, col_tap : col_tap + columns, :
            ].reshape(-1, model_dim)
            conv_sum = conv_sum + jnp.dot(
                window_rows, w_conv[row_tap, col_tap], preferred_element_type=jnp.float32
            )
    hidden = jax.nn.gelu(conv_sum, approximate=True).astype(jnp.bfloat16)
    memory = jnp.dot(hidden, w_out, preferred_element_type=jnp.float32).astype(jnp.bfloat16)
    memory = memory.reshape(frames_dev, rows_dev, columns * mem_dim)
    band_mask = masks.reshape(frames_dev, band_tokens).astype(jnp.bfloat16)
    partial_value = jnp.einsum(
        "ft,ftd->fd",
        band_mask,
        features.reshape(frames_dev, band_tokens, model_dim),
        preferred_element_type=jnp.float32,
    )
    pooled = lax.psum(partial_value, "space")
    normed = (pooled * lax.rsqrt(jnp.mean(pooled * pooled, axis=1, keepdims=True) + 1e-06)).astype(
        jnp.bfloat16
    )
    pointers = jnp.dot(normed, w_ptr, preferred_element_type=jnp.float32).astype(jnp.bfloat16)
    all_pointers = lax.all_gather(pointers, "tm", axis=0, tiled=True)
    hop_count = (MEMS + frames_dev - 1) // frames_dev
    carried = lax.all_gather(memory, "space", axis=1, tiled=True)
    history = jnp.concatenate(
        [fetch_earlier(carried, hop_count), carried[: frames_dev - 1]], axis=0
    )
    grid_tokens = columns * columns
    hist_frames = history.shape[0]
    history = history.reshape(hist_frames, grid_tokens, mem_dim)
    hist_values = jnp.dot(
        history.reshape(-1, mem_dim), w_value, preferred_element_type=jnp.float32
    ).astype(jnp.bfloat16)
    hist_values = hist_values.reshape(hist_frames, grid_tokens, model_dim)
    tpos_keys = jnp.dot(mem_tpos, w_key, preferred_element_type=jnp.float32)
    ptr_tpos_keys = jnp.dot(
        ptr_tpos[::-1].reshape(POINTERS * ptr_tok, mem_dim),
        w_key,
        preferred_element_type=jnp.float32,
    )
    null_key = jnp.dot(
        empty_memory.reshape(1, mem_dim), w_key, preferred_element_type=jnp.float32
    ).astype(jnp.bfloat16)
    null_value = jnp.dot(
        empty_memory.reshape(1, mem_dim), w_value, preferred_element_type=jnp.float32
    ).astype(jnp.bfloat16)
    padded_ptr = jnp.concatenate(
        [jnp.zeros((POINTERS, model_dim), jnp.bfloat16), all_pointers], axis=0
    )
    ptr_offsets = jnp.repeat(jnp.arange(POINTERS, dtype=jnp.int32) - POINTERS, ptr_tok)
    features_f = features.reshape(frames_dev, band_tokens, model_dim).astype(jnp.float32)
    first_frame = lax.axis_index("tm") * frames_dev
    frame = first_frame + 0
    rows_f = features_f[0]
    centred = rows_f - jnp.mean(rows_f, axis=1, keepdims=True)
    query_in = (
        centred * lax.rsqrt(jnp.mean(centred * centred, axis=1, keepdims=True) + 1e-05)
    ).astype(jnp.bfloat16)
    query = (
        jnp.dot(query_in, w_query, preferred_element_type=jnp.float32) * model_dim ** (-0.5)
    ).astype(jnp.bfloat16)
    blocks = []
    for distance in range(1, MEMS + 1):
        slot_index = hop_count * frames_dev - distance
        key_rows = (
            jnp.dot(history[slot_index], w_key, preferred_element_type=jnp.float32)
            + tpos_keys[distance - 1]
        ).astype(jnp.bfloat16)
        blocks.append((key_rows, hist_values[slot_index], frame - distance >= 0))
    window = lax.dynamic_slice_in_dim(padded_ptr, frame, POINTERS, 0)
    ptr_tokens = window.reshape(POINTERS * ptr_tok, mem_dim)
    ptr_keys = (
        jnp.dot(ptr_tokens, w_key, preferred_element_type=jnp.float32) + ptr_tpos_keys
    ).astype(jnp.bfloat16)
    ptr_values = jnp.dot(ptr_tokens, w_value, preferred_element_type=jnp.float32).astype(
        jnp.bfloat16
    )
    extra_valid = jnp.concatenate([frame + ptr_offsets >= 0, jnp.ones((1,), bool)], axis=0)
    blocks.append(
        (
            jnp.concatenate([ptr_keys, null_key], axis=0),
            jnp.concatenate([ptr_values, null_value], axis=0),
            extra_valid[None, :],
        )
    )
    mixed_rows = attend(query, blocks)
    outputs = [
        (rows_f + jnp.dot(mixed_rows, w_proj, preferred_element_type=jnp.float32)).astype(
            jnp.bfloat16
        )
    ]
    attended = jnp.stack(outputs, axis=0).reshape(frames_dev, rows_dev, columns, model_dim)
    return (attended, memory, pointers)


def solution(mesh):
    return jax.shard_map(
        body,
        mesh=mesh,
        in_specs=(
            P("tm", "space", None, None),
            P("tm", "space", None),
            P(),
            P(),
            P(),
            P(),
            P(),
            P(),
            P(),
            P(),
            P(),
            P(),
            P(),
            P(),
        ),
        out_specs=(P("tm", "space", None, None), P("tm", "space", None), P("tm", None)),
        check_vma=False,
    )
```

profile of v0, /device:TPU:24, one launch (start us, length us, event | category | flops | bytes accessed | tf_op | source)
XLA Modules:
  0.0 78.9 jit_solution(8171158523613113094)
XLA Ops:
  0.7 0.7 convert_element_type.111
  1.4 0.8 convert_bitcast_fusion
  2.3 1.0 %fusion.12 = bf16[128,256]{1,0:T(8,128)(2,1)S(1)} fusion(bf16[128,256]{1,0:T(8,128)(2,1)} %bitcast.107, bf16[256,256]{1,0:T(8,128)(2,1)S(1)} %copy-done, f32[256]{0:T(256)S(1)} %convert_element_type.111, f32[128]{0:T(128)S(1)} %convert_element_type.110), kind=kOutput, calls=%fused_computation.29 | convolution fusion | flops 16875520 | bytes 263680 | tf_op jit(solution)/shard_map/dot_general | solution.py:80
  3.3 1.3 %collective-permute-start.1 = (bf16[1,1,16,256]{3,2,1,0:T(8,128)(2,1)S(1)}, bf16[1,1,16,256]{3,2,1,0:T(8,128)(2,1)S(1)}, u32[]{:S(2)}, u32[]{:S(2)}) collective-permute-start(bf16[1,1,16,256]{3,2,1,0:T(8,128)(2,1)S(1)} %get-tuple-element.15), channel_id=1, source_target_pairs={{1,0},{3,2},{5,4},{7,6},{9,8},{11,10},{13,12},{15,14},{17,16},{19,... | collective-permute-start | bytes 24584 | tf_op jit(solution)/shard_map/ppermute | solution.py:24
  4.6 3.0 %collective-permute-start = (bf16[1,1,16,256]{3,2,1,0:T(8,128)(2,1)S(1)}, bf16[1,1,16,256]{3,2,1,0:T(8,128)(2,1)S(1)}, u32[]{:S(2)}, u32[]{:S(2)}) collective-permute-start(bf16[1,1,16,256]{3,2,1,0:T(8,128)(2,1)S(1)} %get-tuple-element.14), channel_id=1, source_target_pairs={{0,1},{2,3},{4,5},{6,7},{8,9},{10,11},{12,13},{14,15},{16,17},{18,... | collective-permute-start | bytes 24584 | tf_op jit(solution)/shard_map/ppermute | solution.py:21
  7.6 0.9 %convert_reduce_fusion = f32[8,16]{1,0:T(8,128)S(1)} fusion(bf16[1,8,16,256]{3,2,1,0:T(8,128)(2,1)} %param.14), kind=kLoop, calls=%fused_computation.42 | loop fusion | flops 65408 | bytes 66048 | tf_op jit(solution)/shard_map/reduce_sum | solution.py:143
  8.6 1.1 %fusion.22 = f32[8,16]{1,0:T(8,128)S(1)} fusion(bf16[1,8,16,256]{3,2,1,0:T(8,128)(2,1)} %param.14, f32[8,16]{1,0:T(8,128)S(1)} %broadcast_multiply_fusion), kind=kLoop, calls=%fused_computation.50 | loop fusion | flops 130944 | bytes 66560 | tf_op jit(solution)/shard_map/reduce_sum | solution.py:145
  9.8 0.9 %fusion.117 = f32[3,256]{1,0:T(4,128)S(1)} fusion(bf16[3,64]{1,0:T(4,128)(2,1)} %param.25, bf16[64,256]{1,0:T(8,128)(2,1)} %param.22), kind=kOutput, calls=%fused_computation.157 | convolution fusion | flops 98304 | bytes 36224 | tf_op jit(solution)/shard_map/dot_general | solution.py:123
  10.8 0.9 %fusion.100 = f32[1,256]{1,0:T(1,128)S(1)} fusion(bf16[64,256]{1,0:T(8,128)(2,1)} %param.22, bf16[64]{0:T(256)(128)(2,1)} %param.27), kind=kOutput, calls=%fused_computation.138 | convolution fusion | flops 32768 | bytes 33920 | tf_op jit(solution)/shard_map/dot_general | solution.py:129
  11.7 1.0 %convolution_bitcast_fusion = f32[1,256]{1,0:T(1,128)S(1)} fusion(bf16[1,8,16,256]{3,2,1,0:T(8,128)(2,1)} %param.14, bf16[8,16,1]{1,0,2:T(8,128)(2,1)S(1)} %get-tuple-element.19), kind=kOutput, calls=%fused_computation.36 | convolution fusion | flops 65536 | bytes 66816 | tf_op jit(solution)/shard_map/ft,ftd->fd/dot_general | solution.py:99
  12.7 2.4 %psum.7 = f32[1,256]{1,0:T(1,128)S(1)} all-reduce(f32[1,256]{1,0:T(1,128)S(1)} %convolution_bitcast_fusion), channel_id=1, replica_groups=mesh['tm'=16,'space'=2] {'space'}, use_global_device_ids=true, to_apply=%region_5.6 | all-reduce | flops 256 | bytes 2048 | tf_op jit(solution)/shard_map/psum | solution.py:105
  15.2 0.6 multiply_reduce_fusion
  16.5 1.0 %fusion.94 = f32[1,256]{1,0:T(1,128)S(1)} fusion(bf16[256,256]{1,0:T(8,128)(2,1)} %param.20, f32[1,256]{1,0:T(1,128)S(1)} %psum.7, f32[]{:T(128)S(6)} %rsqrt.17), kind=kOutput, calls=%fused_computation.131 | convolution fusion | flops 131584 | bytes 133124 | tf_op jit(solution)/shard_map/dot_general | solution.py:109
  17.5 32.6 %all-gather.1 = bf16[16,1,256]{2,1,0:T(2,128)(2,1)S(1)} all-gather(bf16[1,1,256]{2,1,0:T(2,128)(2,1)S(1)} %reshape.203), channel_id=2, replica_groups=mesh['tm'=16,'space'=2] {'tm'}, dimensions={0}, use_global_device_ids=true | all-gather | bytes 8704 | tf_op jit(solution)/shard_map/all_gather | solution.py:110
  50.2 0.9 %fusion.118 = f32[64,256]{1,0:T(8,128)S(1)} fusion(bf16[64,64]{1,0:T(8,128)(2,1)S(1)} %reshape.200, bf16[64,256]{1,0:T(8,128)(2,1)} %param.22), kind=kOutput, calls=%fused_computation.158 | convolution fusion | flops 2097152 | bytes 106496 | tf_op jit(solution)/shard_map/dot_general | solution.py:161
  51.1 0.7 rev.3
  52.1 0.9 %convolution_convert_fusion.1 = bf16[64,256]{1,0:T(8,128)(2,1)S(1)} fusion(bf16[64,64]{1,0:T(8,128)(2,1)S(1)} %reshape.200, bf16[64,256]{1,0:T(8,128)(2,1)} %param.23), kind=kOutput, calls=%fused_computation.33 | convolution fusion | flops 2113536 | bytes 73728 | tf_op jit(solution)/shard_map/dot_general | solution.py:163
  53.0 0.9 %fusion.14 = bf16[64,256]{1,0:T(8,128)(2,1)S(1)} fusion(f32[64,256]{1,0:T(8,128)S(1)} %fusion.118, bf16[64,64]{1,0:T(8,128)(2,1)S(1)} %reshape.201, bf16[64,256]{1,0:T(8,128)(2,1)} %param.22), kind=kOutput, calls=%fused_computation.32 | convolution fusion | flops 2129920 | bytes 139264 | tf_op jit(solution)/shard_map/dot_general | solution.py:124
  54.0 0.2 fusion.11
  54.2 0.2 fusion.113
  54.4 0.1 fusion.98
  54.6 0.2 fusion.35
  54.8 0.2 fusion.45
  55.0 0.2 convolution_add_fusion.13
  55.1 0.2 convolution_add_fusion.12
  55.3 0.2 convolution_add_fusion.11
  55.5 0.2 convolution_add_fusion.10
  55.7 0.2 convolution_add_fusion.9
  55.8 0.2 convolution_add_fusion.8
  56.0 0.3 convolution_convert_fusion.2
  56.6 1.8 %all_gather.6 = bf16[1,16,1024]{2,1,0:T(8,128)(2,1)S(1)} all-gather(bf16[1,8,1024]{2,1,0:T(8,128)(2,1)S(1)} %reshape.196), channel_id=1, replica_groups=mesh['tm'=16,'space'=2] {'space'}, dimensions={1}, use_global_device_ids=true | all-gather | bytes 49152 | tf_op jit(solution)/shard_map/all_gather | solution.py:112
  58.4 3.4 %collective-permute-start.2 = (bf16[1,16,1024]{2,1,0:T(8,128)(2,1)S(1)}, bf16[1,16,1024]{2,1,0:T(8,128)(2,1)S(1)}, u32[]{:S(2)}, u32[]{:S(2)}) collective-permute-start(bf16[1,16,1024]{2,1,0:T(8,128)(2,1)S(1)} %all_gather.6), channel_id=1, source_target_pairs={{0,2},{2,4},{4,6},{6,8},{8,10},{10,12},{12,14},{14,16},{16,18},{18... | collective-permute-start | bytes 98312 | tf_op jit(solution)/shard_map/ppermute | solution.py:13
  61.9 6.1 %collective-permute-start.3 = (bf16[1,16,1024]{2,1,0:T(8,128)(2,1)S(1)}, bf16[1,16,1024]{2,1,0:T(8,128)(2,1)S(1)}, u32[]{:S(2)}, u32[]{:S(2)}) collective-permute-start(bf16[1,16,1024]{2,1,0:T(8,128)(2,1)S(1)} %all_gather.6), channel_id=1, source_target_pairs={{0,4},{2,6},{4,8},{6,10},{8,12},{10,14},{12,16},{14,18},{16,20},{1... | collective-permute-start | bytes 98312 | tf_op jit(solution)/shard_map/ppermute | solution.py:13
  68.0 1.9 %collective-permute-start.4 = (bf16[1,16,1024]{2,1,0:T(8,128)(2,1)S(1)}, bf16[1,16,1024]{2,1,0:T(8,128)(2,1)S(1)}, u32[]{:S(2)}, u32[]{:S(2)}) collective-permute-start(bf16[1,16,1024]{2,1,0:T(8,128)(2,1)S(1)} %all_gather.6), channel_id=1, source_target_pairs={{0,6},{2,8},{4,10},{6,12},{8,14},{10,16},{12,18},{14,20},{16,22},{... | collective-permute-start | bytes 98312 | tf_op jit(solution)/shard_map/ppermute | solution.py:13
  69.9 0.6 convert_element_type.121
  70.5 4.2 %collective-permute-done.4 = bf16[1,16,1024]{2,1,0:T(8,128)(2,1)S(1)} collective-permute-done((bf16[1,16,1024]{2,1,0:T(8,128)(2,1)S(1)}, bf16[1,16,1024]{2,1,0:T(8,128)(2,1)S(1)}, u32[]{:S(2)}, u32[]{:S(2)}) %collective-permute-start.4) | collective-permute-done | bytes 32800 | tf_op jit(solution)/shard_map/ppermute | solution.py:13
  74.7 0.2 reshape_reshape.3
  74.9 0.2 convolution_convert_fusion
  75.2 0.4 fusion.115
  75.6 0.1 squeeze.51
  75.8 0.4 fusion.114
  76.3 0.4 fusion.116
  76.8 0.2 fusion.63
  77.1 0.2 fusion.33
  77.3 0.2 convolution_add_fusion.6
  77.5 0.2 convolution_add_fusion.5
  77.8 0.2 copy-done.5
  78.0 1.0 %fusion.13 = bf16[128,256]{1,0:T(8,128)(2,1)} fusion(bf16[256,256]{1,0:T(8,128)(2,1)S(1)} %copy-done.5, f32[128,256]{1,0:T(8,128)S(1)} %convolution_add_fusion.5, bf16[128,256]{1,0:T(8,128)(2,1)S(1)} %bitcast.109, bf16[1,256]{1,0:T(2,128)(2,1)S(1)} %convert_element_type.132, bf16[64,256]{1,0:T(8,128)(2,1)S(1)} %convolution_convert_fusion.1, ...), kind=kOutput, calls=%fused_computation.30 | convolution fusion | flops 21292416 | bytes 460800 | tf_op jit(solution)/shard_map/dot_general | solution.py:176
  (55 shorter events, 1.4 us)
Async XLA Ops:
  0.6 1.6 %copy-start = (bf16[256,256]{1,0:T(8,128)(2,1)S(1)}, bf16[256,256]{1,0:T(8,128)(2,1)}, u32[]{:S(2)}) copy-start(bf16[256,256]{1,0:T(8,128)(2,1)} %param.16) | copy-start | bytes 393220
  0.6 53.3 %copy-start.2 = (bf16[1,8,16,256]{3,2,1,0:T(8,128)(2,1)S(1)}, bf16[1,8,16,256]{3,2,1,0:T(8,128)(2,1)}, u32[]{:S(2)}) copy-start(bf16[1,8,16,256]{3,2,1,0:T(8,128)(2,1)} %param.14) | copy-start | bytes 196612
  0.7 53.7 %copy-start.7 = (bf16[64]{0:T(256)(128)(2,1)S(1)}, bf16[64]{0:T(256)(128)(2,1)}, u32[]{:S(2)}) copy-start(bf16[64]{0:T(256)(128)(2,1)} %param.27) | copy-start | bytes 388
  0.7 53.7 %copy-start.4 = (bf16[64,256]{1,0:T(8,128)(2,1)S(1)}, bf16[64,256]{1,0:T(8,128)(2,1)}, u32[]{:S(2)}) copy-start(bf16[64,256]{1,0:T(8,128)(2,1)} %param.23) | copy-start | bytes 98308
  0.7 53.3 %copy-start.8 = (bf16[256,256]{1,0:T(8,128)(2,1)S(1)}, bf16[256,256]{1,0:T(8,128)(2,1)}, u32[]{:S(2)}) copy-start(bf16[256,256]{1,0:T(8,128)(2,1)} %param.21) | copy-start | bytes 393220
  3.3 51.2 %collective-permute-start.1 = (bf16[1,1,16,256]{3,2,1,0:T(8,128)(2,1)S(1)}, bf16[1,1,16,256]{3,2,1,0:T(8,128)(2,1)S(1)}, u32[]{:S(2)}, u32[]{:S(2)}) collective-permute-start(bf16[1,1,16,256]{3,2,1,0:T(8,128)(2,1)S(1)} %get-tuple-element.15), channel_id=1, source_target_pairs={{1,0},{3,2},{5,4},{7,6},{9,8},{11,10},{13,12},{15,14},{17,16},{19,... | collective-permute-start | bytes 24584 | tf_op jit(solution)/shard_map/ppermute | solution.py:24
  4.6 49.9 %collective-permute-start = (bf16[1,1,16,256]{3,2,1,0:T(8,128)(2,1)S(1)}, bf16[1,1,16,256]{3,2,1,0:T(8,128)(2,1)S(1)}, u32[]{:S(2)}, u32[]{:S(2)}) collective-permute-start(bf16[1,1,16,256]{3,2,1,0:T(8,128)(2,1)S(1)} %get-tuple-element.14), channel_id=1, source_target_pairs={{0,1},{2,3},{4,5},{6,7},{8,9},{10,11},{12,13},{14,15},{16,17},{18,... | collective-permute-start | bytes 24584 | tf_op jit(solution)/shard_map/ppermute | solution.py:21
  8.6 46.0 %copy-start.3 = (bf16[3,3,256,256]{3,2,1,0:T(8,128)(2,1)S(1)}, bf16[3,3,256,256]{3,2,1,0:T(8,128)(2,1)}, u32[]{:S(2)}) copy-start(bf16[3,3,256,256]{3,2,1,0:T(8,128)(2,1)} %param.18) | copy-start | bytes 3538948
  55.1 0.9 %copy-start.9 = (bf16[256,64]{0,1:T(8,128)(2,1)S(1)}, bf16[256,64]{0,1:T(8,128)(2,1)}, u32[]{:S(2)}) copy-start(bf16[256,64]{0,1:T(8,128)(2,1)} %param.19) | copy-start | bytes 98308
  55.8 19.4 %copy-start.1 = (bf16[64,256]{1,0:T(8,128)(2,1)S(1)}, bf16[64,256]{1,0:T(8,128)(2,1)}, u32[]{:S(2)}) copy-start(bf16[64,256]{1,0:T(8,128)(2,1)} %param.22) | copy-start | bytes 98308
  56.6 20.2 %copy-start.6 = (bf16[1,8,1024]{2,1,0:T(8,128)(2,1)}, bf16[1,8,1024]{2,1,0:T(8,128)(2,1)S(1)}, u32[]{:S(2)}) copy-start(bf16[1,8,1024]{2,1,0:T(8,128)(2,1)S(1)} %reshape.196) | copy-start | bytes 49156
  58.4 12.0 %collective-permute-start.2 = (bf16[1,16,1024]{2,1,0:T(8,128)(2,1)S(1)}, bf16[1,16,1024]{2,1,0:T(8,128)(2,1)S(1)}, u32[]{:S(2)}, u32[]{:S(2)}) collective-permute-start(bf16[1,16,1024]{2,1,0:T(8,128)(2,1)S(1)} %all_gather.6), channel_id=1, source_target_pairs={{0,2},{2,4},{4,6},{6,8},{8,10},{10,12},{12,14},{14,16},{16,18},{18... | collective-permute-start | bytes 98312 | tf_op jit(solution)/shard_map/ppermute | solution.py:13
  61.9 8.6 %collective-permute-start.3 = (bf16[1,16,1024]{2,1,0:T(8,128)(2,1)S(1)}, bf16[1,16,1024]{2,1,0:T(8,128)(2,1)S(1)}, u32[]{:S(2)}, u32[]{:S(2)}) collective-permute-start(bf16[1,16,1024]{2,1,0:T(8,128)(2,1)S(1)} %all_gather.6), channel_id=1, source_target_pairs={{0,4},{2,6},{4,8},{6,10},{8,12},{10,14},{12,16},{14,18},{16,20},{1... | collective-permute-start | bytes 98312 | tf_op jit(solution)/shard_map/ppermute | solution.py:13
  68.0 6.7 %collective-permute-start.4 = (bf16[1,16,1024]{2,1,0:T(8,128)(2,1)S(1)}, bf16[1,16,1024]{2,1,0:T(8,128)(2,1)S(1)}, u32[]{:S(2)}, u32[]{:S(2)}) collective-permute-start(bf16[1,16,1024]{2,1,0:T(8,128)(2,1)S(1)} %all_gather.6), channel_id=1, source_target_pairs={{0,6},{2,8},{4,10},{6,12},{8,14},{10,16},{12,18},{14,20},{16,22},{... | collective-permute-start | bytes 98312 | tf_op jit(solution)/shard_map/ppermute | solution.py:13
  77.0 0.9 %copy-start.5 = (bf16[256,256]{1,0:T(8,128)(2,1)S(1)}, bf16[256,256]{1,0:T(8,128)(2,1)}, u32[]{:S(2)}) copy-start(bf16[256,256]{1,0:T(8,128)(2,1)} %param.24) | copy-start | bytes 393220
where the time goes:
time: 79.8 us; the launch traced here: 78.9 us
  blocking collectives  36.9 us (46%)
  starting transfers between devices  15.7 us (20%)
  matrix products  12.9 us (16%)
  other arithmetic  4.59 us (6%)
  waiting for transfers between devices  4.19 us (5%)
  local copies, waits for them, and re-layouts  2.96 us (4%)
  between operations  1.72 us (2%)
    all_gather x1, blocking collectives, body(): all_pointers = lax.all_gather(pointers, 'tm', axis=0, tiled=True)  32.6 us
    ppermute x3, starting transfers between devices, from_behind(): return lax.ppermute(block, axis, route)  11.4 us
    ppermute x3, waiting for transfers between devices, from_behind(): return lax.ppermute(block, axis, route)  4.18 us
    ppermute x1, starting transfers between devices, with_halo(): lax.ppermute(lax.slice_in_dim(block, block.shape[dim] - width, None, axis...  3.03 us
    psum x1, blocking collectives, body(): pooled = lax.psum(partial_value, 'space')  2.45 us
    all_gather x1, blocking collectives, body(): carried = lax.all_gather(memory, 'space', axis=1, tiled=True)  1.83 us
  transfers between devices with their start and end apart: 5, of which 1 were waited for; matrix products, arithmetic and copies ran while one was open for 15% of the time, Pallas kernels for 0%

commit v1 on v0

--- a/solution.py
+++ b/solution.py
@@ -5,6 +5,18 @@
 
 MEMS = 3
 POINTERS = 16
+
+
+def doubled_up(value, axis, dim):
+    ways, here, step = (lax.axis_size(axis), lax.axis_index(axis), value.shape[dim])
+    line, have = (value, 1)
+    while have < ways:
+        line = jnp.concatenate(
+            [line, lax.ppermute(line, axis, [(d, (d - have) % ways) for d in range(ways)])],
+            axis=dim,
+        )
+        have = 2 * have
+    return jnp.roll(line, here * step, axis=dim)
 
 
 def from_behind(block, axis, distance):
@@ -107,7 +119,7 @@
         jnp.bfloat16
     )
     pointers = jnp.dot(normed, w_ptr, preferred_element_type=jnp.float32).astype(jnp.bfloat16)
-    all_pointers = lax.all_gather(pointers, "tm", axis=0, tiled=True)
+    all_pointers = doubled_up(pointers, "tm", 0)
     hop_count = (MEMS + frames_dev - 1) // frames_dev
     carried = lax.all_gather(memory, "space", axis=1, tiled=True)
     history = jnp.concatenate(

time: 79.8 us -> 61 us (0.76)
  the two profiles are of different devices: /device:TPU:24 before, /device:TPU:0 now
where the time goes in v1:
time: 61 us; the launch traced here: 60.2 us
  starting transfers between devices  23.7 us (39%)
  matrix products  12.3 us (20%)
  waiting for transfers between devices  11.7 us (19%)
  other arithmetic  4.51 us (7%)
  blocking collectives  4.41 us (7%)
  local copies, waits for them, and re-layouts  1.83 us (3%)
  between operations  1.75 us (3%)
    ppermute x3, starting transfers between devices, from_behind(): return lax.ppermute(block, axis, route)  11.3 us
    ppermute x4, waiting for transfers between devices, doubled_up(): lax.ppermute(line, axis, [(d, (d - have) % ways) for d in range(ways)])  10.2 us
    ppermute x4, starting transfers between devices, doubled_up(): lax.ppermute(line, axis, [(d, (d - have) % ways) for d in range(ways)])  8.14 us
    ppermute x1, starting transfers between devices, with_halo(): lax.ppermute(lax.slice_in_dim(block, block.shape[dim] - width, None, axis...  3.03 us
    psum x1, blocking collectives, body(): pooled = lax.psum(partial_value, 'space')  2.58 us
    all_gather x1, blocking collectives, body(): carried = lax.all_gather(memory, 'space', axis=1, tiled=True)  1.83 us
    dot_general x4, matrix products, attend(): lax.dot_general(query, key_rows, (((1,), (1,)), ((), ())), preferred_elem...  1.45 us
    ppermute x3, waiting for transfers between devices, from_behind(): return lax.ppermute(block, axis, route)  1.44 us
  transfers between devices with their start and end apart: 9, of which 4 were waited for; matrix products, arithmetic and copies ran while one was open for 16% of the time, Pallas kernels for 0%

profile of v1, /device:TPU:0, one launch (start us, length us, event | category | flops | bytes accessed | tf_op | source)
XLA Modules:
  0.0 60.2 jit_solution(15603972470256879242)
XLA Ops:
  0.7 0.7 %convert_element_type.111 = f32[256]{0:T(256)S(1)} convert(bf16[256]{0:T(256)(128)(2,1)} %param.17) | non-fusion elementwise | flops 256 | bytes 1536 | tf_op jit(solution)/shard_map/convert_element_type | solution.py:93
  1.4 0.8 %convert_bitcast_fusion = (bf16[8,16,1]{1,0,2:T(8,128)(2,1)S(1)}, f32[1,8,16]{2,1,0:T(8,128)S(1)}) fusion(s32[1,8,16]{2,1,0:T(8,128)} %param.15), kind=kLoop, calls=%fused_computation.129 | loop fusion | flops 256 | bytes 1280 | tf_op jit(solution)/shard_map/reshape.131
  2.2 1.0 %fusion.12 = bf16[128,256]{1,0:T(8,128)(2,1)S(1)} fusion(bf16[128,256]{1,0:T(8,128)(2,1)} %bitcast.104, bf16[256,256]{1,0:T(8,128)(2,1)S(1)} %copy-done, f32[256]{0:T(256)S(1)} %convert_element_type.111, f32[128]{0:T(128)S(1)} %convert_element_type.110), kind=kOutput, calls=%fused_computation.29 | convolution fusion | flops 16875520 | bytes 263680 | tf_op jit(solution)/shard_map/dot_general | solution.py:92
  3.2 1.3 %collective-permute-start.1 = (bf16[1,1,16,256]{3,2,1,0:T(8,128)(2,1)S(1)}, bf16[1,1,16,256]{3,2,1,0:T(8,128)(2,1)S(1)}, u32[]{:S(2)}, u32[]{:S(2)}) collective-permute-start(bf16[1,1,16,256]{3,2,1,0:T(8,128)(2,1)S(1)} %get-tuple-element.15), channel_id=1, source_target_pairs={{1,0},{3,2},{5,4},{7,6},{9,8},{11,10},{13,12},{15,14},{17,16},{19,... | collective-permute-start | bytes 24584 | tf_op jit(solution)/shard_map/ppermute | solution.py:36
  4.5 3.0 %collective-permute-start = (bf16[1,1,16,256]{3,2,1,0:T(8,128)(2,1)S(1)}, bf16[1,1,16,256]{3,2,1,0:T(8,128)(2,1)S(1)}, u32[]{:S(2)}, u32[]{:S(2)}) collective-permute-start(bf16[1,1,16,256]{3,2,1,0:T(8,128)(2,1)S(1)} %get-tuple-element.14), channel_id=1, source_target_pairs={{0,1},{2,3},{4,5},{6,7},{8,9},{10,11},{12,13},{14,15},{16,17},{18,... | collective-permute-start | bytes 24584 | tf_op jit(solution)/shard_map/ppermute | solution.py:33
  7.6 1.0 %convolution_bitcast_fusion = f32[1,256]{1,0:T(1,128)S(1)} fusion(bf16[1,8,16,256]{3,2,1,0:T(8,128)(2,1)} %param.14, bf16[8,16,1]{1,0,2:T(8,128)(2,1)S(1)} %get-tuple-element.19), kind=kOutput, calls=%fused_computation.36 | convolution fusion | flops 65536 | bytes 66816 | tf_op jit(solution)/shard_map/ft,ftd->fd/dot_general | solution.py:111
  8.6 2.6 %psum.7 = f32[1,256]{1,0:T(1,128)S(1)} all-reduce(f32[1,256]{1,0:T(1,128)S(1)} %convolution_bitcast_fusion), channel_id=1, replica_groups=mesh['tm'=16,'space'=2] {'space'}, use_global_device_ids=true, to_apply=%region_5.6 | all-reduce | flops 256 | bytes 2048 | tf_op jit(solution)/shard_map/psum | solution.py:117
  11.2 0.6 %multiply_reduce_fusion = f32[]{:T(128)} fusion(f32[1,256]{1,0:T(1,128)S(1)} %psum.7), kind=kLoop, calls=%fused_computation.137 | loop fusion | flops 511 | bytes 1028 | tf_op jit(solution)/shard_map/reduce_sum | solution.py:118
  12.5 1.0 %fusion.94 = f32[1,256]{1,0:T(1,128)S(1)} fusion(bf16[256,256]{1,0:T(8,128)(2,1)} %param.20, f32[1,256]{1,0:T(1,128)S(1)} %psum.7, f32[]{:T(128)S(6)} %rsqrt.17), kind=kOutput, calls=%fused_computation.133 | convolution fusion | flops 131584 | bytes 133124 | tf_op jit(solution)/shard_map/dot_general | solution.py:121
  13.6 7.0 %collective-permute-start.5 = (bf16[1,256]{1,0:T(2,128)(2,1)S(1)}, bf16[1,256]{1,0:T(2,128)(2,1)S(1)}, u32[]{:S(2)}, u32[]{:S(2)}) collective-permute-start(bf16[1,256]{1,0:T(2,128)(2,1)S(1)} %convert_element_type.121), channel_id=1, source_target_pairs={{0,30},{2,0},{4,2},{6,4},{8,6},{10,8},{12,10},{14,12},{16,14},{18,... | collective-permute-start | bytes 1544 | tf_op jit(solution)/shard_map/ppermute | solution.py:15
  20.6 0.9 %convert_reduce_fusion = f32[8,16]{1,0:T(8,128)S(1)} fusion(bf16[1,8,16,256]{3,2,1,0:T(8,128)(2,1)} %param.14), kind=kLoop, calls=%fused_computation.42 | loop fusion | flops 65408 | bytes 66048 | tf_op jit(solution)/shard_map/reduce_sum | solution.py:155
  21.5 1.0 %fusion.22 = f32[8,16]{1,0:T(8,128)S(1)} fusion(bf16[1,8,16,256]{3,2,1,0:T(8,128)(2,1)} %param.14, f32[8,16]{1,0:T(8,128)S(1)} %broadcast_multiply_fusion), kind=kLoop, calls=%fused_computation.50 | loop fusion | flops 130944 | bytes 66560 | tf_op jit(solution)/shard_map/reduce_sum | solution.py:157
  22.7 0.9 %fusion.117 = f32[3,256]{1,0:T(4,128)S(1)} fusion(bf16[3,64]{1,0:T(4,128)(2,1)} %param.25, bf16[64,256]{1,0:T(8,128)(2,1)} %param.22), kind=kOutput, calls=%fused_computation.160 | convolution fusion | flops 98304 | bytes 36224 | tf_op jit(solution)/shard_map/dot_general | solution.py:135
  23.6 0.9 %fusion.100 = f32[1,256]{1,0:T(1,128)S(1)} fusion(bf16[64,256]{1,0:T(8,128)(2,1)} %param.22, bf16[64]{0:T(256)(128)(2,1)} %param.27), kind=kOutput, calls=%fused_computation.140 | convolution fusion | flops 32768 | bytes 33920 | tf_op jit(solution)/shard_map/dot_general | solution.py:141
  24.5 1.2 %fusion.11 = bf16[128,256]{1,0:T(8,128)(2,1)S(1)} fusion(bf16[256,256]{1,0:T(8,128)(2,1)} %param.21, bf16[128,256]{1,0:T(8,128)(2,1)} %bitcast.105, f32[128]{0:T(128)S(1)} %rsqrt.16, f32[128]{0:T(128)S(1)} %div.40), kind=kOutput, calls=%fused_computation.28 | convolution fusion | flops 16973824 | bytes 263168 | tf_op jit(solution)/shard_map/dot_general | solution.py:160
  25.7 0.9 %fusion.98 = f32[1,256]{1,0:T(1,128)S(1)} fusion(bf16[64,256]{1,0:T(8,128)(2,1)} %param.23, bf16[64]{0:T(256)(128)(2,1)} %param.27), kind=kOutput, calls=%fused_computation.138 | convolution fusion | flops 32768 | bytes 33920 | tf_op jit(solution)/shard_map/dot_general | solution.py:144
  26.6 0.6 collective-permute-start.6
  27.2 3.1 %collective-permute-done.6 = bf16[2,256]{1,0:T(2,128)(2,1)S(1)} collective-permute-done((bf16[2,256]{1,0:T(2,128)(2,1)S(1)}, bf16[2,256]{1,0:T(2,128)(2,1)S(1)}, u32[]{:S(2)}, u32[]{:S(2)}) %collective-permute-start.6) | collective-permute-done | bytes 1056 | tf_op jit(solution)/shard_map/ppermute | solution.py:15
  30.2 0.5 collective-permute-start.7
  30.9 3.0 %collective-permute-done.7 = bf16[4,256]{1,0:T(4,128)(2,1)S(1)} collective-permute-done((bf16[4,256]{1,0:T(4,128)(2,1)S(1)}, bf16[4,256]{1,0:T(4,128)(2,1)S(1)}, u32[]{:S(2)}, u32[]{:S(2)}) %collective-permute-start.7) | collective-permute-done | bytes 2080 | tf_op jit(solution)/shard_map/ppermute | solution.py:15
  34.2 4.2 %collective-permute-done.8 = bf16[8,256]{1,0:T(8,128)(2,1)S(1)} collective-permute-done((bf16[8,256]{1,0:T(8,128)(2,1)S(1)}, bf16[8,256]{1,0:T(8,128)(2,1)S(1)}, u32[]{:S(2)}, u32[]{:S(2)}) %collective-permute-start.8) | collective-permute-done | bytes 4128 | tf_op jit(solution)/shard_map/ppermute | solution.py:15
  38.6 0.1 fusion.118
  38.8 0.1 fusion.14
  38.9 0.2 fusion.113
  39.2 0.2 fusion.35
  39.4 0.2 fusion.45
  39.6 0.2 convolution_add_fusion.13
  39.7 0.2 convolution_add_fusion.12
  39.9 0.2 convolution_add_fusion.11
  40.1 0.2 convolution_add_fusion.10
  40.3 0.2 convolution_add_fusion.9
  40.4 0.2 convolution_add_fusion.8
  40.6 0.3 convolution_convert_fusion.2
  41.2 1.8 %all_gather.3 = bf16[1,16,1024]{2,1,0:T(8,128)(2,1)S(1)} all-gather(bf16[1,8,1024]{2,1,0:T(8,128)(2,1)S(1)} %reshape.196), channel_id=1, replica_groups=mesh['tm'=16,'space'=2] {'space'}, dimensions={1}, use_global_device_ids=true | all-gather | bytes 49152 | tf_op jit(solution)/shard_map/all_gather | solution.py:124
  43.0 1.3 %collective-permute-start.2 = (bf16[1,16,1024]{2,1,0:T(8,128)(2,1)S(1)}, bf16[1,16,1024]{2,1,0:T(8,128)(2,1)S(1)}, u32[]{:S(2)}, u32[]{:S(2)}) collective-permute-start(bf16[1,16,1024]{2,1,0:T(8,128)(2,1)S(1)} %all_gather.3), channel_id=1, source_target_pairs={{0,2},{2,4},{4,6},{6,8},{8,10},{10,12},{12,14},{14,16},{16,18},{18... | collective-permute-start | bytes 98312 | tf_op jit(solution)/shard_map/ppermute | solution.py:25
  44.4 5.2 %collective-permute-start.3 = (bf16[1,16,1024]{2,1,0:T(8,128)(2,1)S(1)}, bf16[1,16,1024]{2,1,0:T(8,128)(2,1)S(1)}, u32[]{:S(2)}, u32[]{:S(2)}) collective-permute-start(bf16[1,16,1024]{2,1,0:T(8,128)(2,1)S(1)} %all_gather.3), channel_id=1, source_target_pairs={{0,4},{2,6},{4,8},{6,10},{8,12},{10,14},{12,16},{14,18},{16,20},{1... | collective-permute-start | bytes 98312 | tf_op jit(solution)/shard_map/ppermute | solution.py:25
  49.6 4.8 %collective-permute-start.4 = (bf16[1,16,1024]{2,1,0:T(8,128)(2,1)S(1)}, bf16[1,16,1024]{2,1,0:T(8,128)(2,1)S(1)}, u32[]{:S(2)}, u32[]{:S(2)}) collective-permute-start(bf16[1,16,1024]{2,1,0:T(8,128)(2,1)S(1)} %all_gather.3), channel_id=1, source_target_pairs={{0,6},{2,8},{4,10},{6,12},{8,14},{10,16},{12,18},{14,20},{16,22},{... | collective-permute-start | bytes 98312 | tf_op jit(solution)/shard_map/ppermute | solution.py:25
  54.5 1.4 %collective-permute-done.4 = bf16[1,16,1024]{2,1,0:T(8,128)(2,1)S(1)} collective-permute-done((bf16[1,16,1024]{2,1,0:T(8,128)(2,1)S(1)}, bf16[1,16,1024]{2,1,0:T(8,128)(2,1)S(1)}, u32[]{:S(2)}, u32[]{:S(2)}) %collective-permute-start.4) | collective-permute-done | bytes 32800 | tf_op jit(solution)/shard_map/ppermute | solution.py:25
  55.9 0.2 reshape_reshape.3
  56.1 0.2 convolution_convert_fusion
  56.5 0.4 fusion.115
  57.0 0.4 fusion.114
  57.6 0.4 fusion.116
  58.1 0.2 fusion.63
  58.3 0.2 fusion.33
  58.6 0.2 convolution_add_fusion.6
  58.8 0.2 convolution_add_fusion.5
  59.3 1.0 %fusion.13 = bf16[128,256]{1,0:T(8,128)(2,1)} fusion(bf16[256,256]{1,0:T(8,128)(2,1)S(1)} %copy-done.5, f32[128,256]{1,0:T(8,128)S(1)} %convolution_add_fusion.5, bf16[128,256]{1,0:T(8,128)(2,1)S(1)} %bitcast.106, bf16[1,256]{1,0:T(2,128)(2,1)S(1)} %convert_element_type.132, bf16[64,256]{1,0:T(8,128)(2,1)S(1)} %convolution_convert_fusion.1, ...), kind=kOutput, calls=%fused_computation.30 | convolution fusion | flops 21292416 | bytes 460800 | tf_op jit(solution)/shard_map/dot_general | solution.py:188
  (65 shorter events, 2.1 us)
Async XLA Ops:
  0.6 1.6 %copy-start = (bf16[256,256]{1,0:T(8,128)(2,1)S(1)}, bf16[256,256]{1,0:T(8,128)(2,1)}, u32[]{:S(2)}) copy-start(bf16[256,256]{1,0:T(8,128)(2,1)} %param.16) | copy-start | bytes 393220
  0.6 38.0 %copy-start.1 = (bf16[64,256]{1,0:T(8,128)(2,1)S(1)}, bf16[64,256]{1,0:T(8,128)(2,1)}, u32[]{:S(2)}) copy-start(bf16[64,256]{1,0:T(8,128)(2,1)} %param.22) | copy-start | bytes 98308
  0.7 33.4 %copy-start.8 = (bf16[16,256]{1,0:T(8,128)(2,1)S(1)}, bf16[16,256]{1,0:T(8,128)(2,1)}, u32[]{:S(2)}) copy-start(bf16[16,256]{1,0:T(8,128)(2,1)} %param.26) | copy-start | bytes 24580
  3.2 35.8 %collective-permute-start.1 = (bf16[1,1,16,256]{3,2,1,0:T(8,128)(2,1)S(1)}, bf16[1,1,16,256]{3,2,1,0:T(8,128)(2,1)S(1)}, u32[]{:S(2)}, u32[]{:S(2)}) collective-permute-start(bf16[1,1,16,256]{3,2,1,0:T(8,128)(2,1)S(1)} %get-tuple-element.15), channel_id=1, source_target_pairs={{1,0},{3,2},{5,4},{7,6},{9,8},{11,10},{13,12},{15,14},{17,16},{19,... | collective-permute-start | bytes 24584 | tf_op jit(solution)/shard_map/ppermute | solution.py:36
  4.5 34.5 %collective-permute-start = (bf16[1,1,16,256]{3,2,1,0:T(8,128)(2,1)S(1)}, bf16[1,1,16,256]{3,2,1,0:T(8,128)(2,1)S(1)}, u32[]{:S(2)}, u32[]{:S(2)}) collective-permute-start(bf16[1,1,16,256]{3,2,1,0:T(8,128)(2,1)S(1)} %get-tuple-element.14), channel_id=1, source_target_pairs={{0,1},{2,3},{4,5},{6,7},{8,9},{10,11},{12,13},{14,15},{16,17},{18,... | collective-permute-start | bytes 24584 | tf_op jit(solution)/shard_map/ppermute | solution.py:33
  8.6 30.6 %copy-start.3 = (bf16[3,3,256,256]{3,2,1,0:T(8,128)(2,1)S(1)}, bf16[3,3,256,256]{3,2,1,0:T(8,128)(2,1)}, u32[]{:S(2)}) copy-start(bf16[3,3,256,256]{3,2,1,0:T(8,128)(2,1)} %param.18) | copy-start | bytes 3538948
  13.6 25.8 %copy-start.7 = (bf16[1,256]{1,0:T(2,128)(2,1)}, bf16[1,256]{1,0:T(2,128)(2,1)S(1)}, u32[]{:S(2)}) copy-start(bf16[1,256]{1,0:T(2,128)(2,1)S(1)} %convert_element_type.121) | copy-start | bytes 1540
  13.6 13.0 %collective-permute-start.5 = (bf16[1,256]{1,0:T(2,128)(2,1)S(1)}, bf16[1,256]{1,0:T(2,128)(2,1)S(1)}, u32[]{:S(2)}, u32[]{:S(2)}) collective-permute-start(bf16[1,256]{1,0:T(2,128)(2,1)S(1)} %convert_element_type.121), channel_id=1, source_target_pairs={{0,30},{2,0},{4,2},{6,4},{8,6},{10,8},{12,10},{14,12},{16,14},{18,... | collective-permute-start | bytes 1544 | tf_op jit(solution)/shard_map/ppermute | solution.py:15
  26.6 3.6 %collective-permute-start.6 = (bf16[2,256]{1,0:T(2,128)(2,1)S(1)}, bf16[2,256]{1,0:T(2,128)(2,1)S(1)}, u32[]{:S(2)}, u32[]{:S(2)}) collective-permute-start(bf16[2,256]{1,0:T(2,128)(2,1)S(1)} %pad_maximum_fusion.5), channel_id=1, source_target_pairs={{0,28},{2,30},{4,0},{6,2},{8,4},{10,6},{12,8},{14,10},{16,12},{18,... | collective-permute-start | bytes 3080 | tf_op jit(solution)/shard_map/ppermute | solution.py:15
  30.2 3.6 %collective-permute-start.7 = (bf16[4,256]{1,0:T(4,128)(2,1)S(1)}, bf16[4,256]{1,0:T(4,128)(2,1)S(1)}, u32[]{:S(2)}, u32[]{:S(2)}) collective-permute-start(bf16[4,256]{1,0:T(4,128)(2,1)S(1)} %pad_maximum_fusion.4), channel_id=1, source_target_pairs={{0,24},{2,26},{4,28},{6,30},{8,0},{10,2},{12,4},{14,6},{16,8},{18,... | collective-permute-start | bytes 6152 | tf_op jit(solution)/shard_map/ppermute | solution.py:15
  33.9 4.6 %collective-permute-start.8 = (bf16[8,256]{1,0:T(8,128)(2,1)S(1)}, bf16[8,256]{1,0:T(8,128)(2,1)S(1)}, u32[]{:S(2)}, u32[]{:S(2)}) collective-permute-start(bf16[8,256]{1,0:T(8,128)(2,1)S(1)} %pad_maximum_fusion.3), channel_id=1, source_target_pairs={{0,16},{2,18},{4,20},{6,22},{8,24},{10,26},{12,28},{14,30},{16,0},... | collective-permute-start | bytes 12296 | tf_op jit(solution)/shard_map/ppermute | solution.py:15
  39.7 0.9 %copy-start.9 = (bf16[256,64]{0,1:T(8,128)(2,1)S(1)}, bf16[256,64]{0,1:T(8,128)(2,1)}, u32[]{:S(2)}) copy-start(bf16[256,64]{0,1:T(8,128)(2,1)} %param.19) | copy-start | bytes 98308
  39.9 14.4 %copy-start.4 = (bf16[64,256]{1,0:T(8,128)(2,1)S(1)}, bf16[64,256]{1,0:T(8,128)(2,1)}, u32[]{:S(2)}) copy-start(bf16[64,256]{1,0:T(8,128)(2,1)} %param.23) | copy-start | bytes 98308
  41.2 16.8 %copy-start.6 = (bf16[1,8,1024]{2,1,0:T(8,128)(2,1)}, bf16[1,8,1024]{2,1,0:T(8,128)(2,1)S(1)}, u32[]{:S(2)}) copy-start(bf16[1,8,1024]{2,1,0:T(8,128)(2,1)S(1)} %reshape.196) | copy-start | bytes 49156
  43.0 11.4 %collective-permute-start.2 = (bf16[1,16,1024]{2,1,0:T(8,128)(2,1)S(1)}, bf16[1,16,1024]{2,1,0:T(8,128)(2,1)S(1)}, u32[]{:S(2)}, u32[]{:S(2)}) collective-permute-start(bf16[1,16,1024]{2,1,0:T(8,128)(2,1)S(1)} %all_gather.3), channel_id=1, source_target_pairs={{0,2},{2,4},{4,6},{6,8},{8,10},{10,12},{12,14},{14,16},{16,18},{18... | collective-permute-start | bytes 98312 | tf_op jit(solution)/shard_map/ppermute | solution.py:25
  44.4 10.1 %collective-permute-start.3 = (bf16[1,16,1024]{2,1,0:T(8,128)(2,1)S(1)}, bf16[1,16,1024]{2,1,0:T(8,128)(2,1)S(1)}, u32[]{:S(2)}, u32[]{:S(2)}) collective-permute-start(bf16[1,16,1024]{2,1,0:T(8,128)(2,1)S(1)} %all_gather.3), channel_id=1, source_target_pairs={{0,4},{2,6},{4,8},{6,10},{8,12},{10,14},{12,16},{14,18},{16,20},{1... | collective-permute-start | bytes 98312 | tf_op jit(solution)/shard_map/ppermute | solution.py:25
  49.6 6.3 %collective-permute-start.4 = (bf16[1,16,1024]{2,1,0:T(8,128)(2,1)S(1)}, bf16[1,16,1024]{2,1,0:T(8,128)(2,1)S(1)}, u32[]{:S(2)}, u32[]{:S(2)}) collective-permute-start(bf16[1,16,1024]{2,1,0:T(8,128)(2,1)S(1)} %all_gather.3), channel_id=1, source_target_pairs={{0,6},{2,8},{4,10},{6,12},{8,14},{10,16},{12,18},{14,20},{16,22},{... | collective-permute-start | bytes 98312 | tf_op jit(solution)/shard_map/ppermute | solution.py:25
  58.3 0.8 %copy-start.2 = (bf16[1,8,16,256]{3,2,1,0:T(8,128)(2,1)S(1)}, bf16[1,8,16,256]{3,2,1,0:T(8,128)(2,1)}, u32[]{:S(2)}) copy-start(bf16[1,8,16,256]{3,2,1,0:T(8,128)(2,1)} %param.14) | copy-start | bytes 196612
  58.3 0.9 %copy-start.5 = (bf16[256,256]{1,0:T(8,128)(2,1)S(1)}, bf16[256,256]{1,0:T(8,128)(2,1)}, u32[]{:S(2)}) copy-start(bf16[256,256]{1,0:T(8,128)(2,1)} %param.24) | copy-start | bytes 393220
